TPU v7x, 32 devices: a whole 2x2x4 slice. The times are simulated.
32 devices in a mesh: dp: 8 (over y, x, core), chan: 4 (over z).
Axes of the slice: x: 2, y: 2, z: 4, core: 2. Of those that a mesh axis runs over, the one named last changes fastest.
Arguments:
- patches: bfloat16 [64, 256, 1280], P('dp', None, 'chan'), may hold values from -13 to 13
- cotangent: bfloat16 [64, 256, 1280], P('dp', None, 'chan'), may hold values from -33 to 33
- w_token_in: bfloat16 [640, 256], replicated, may hold values from -0.375 to 0.375
- b_token_in: float32 [640], replicated, may hold values from -3 to 3
- w_token_out: bfloat16 [256, 640], replicated, may hold values from -0.25 to 0.25
- layer_norm_gain: float32 [1280], replicated, may hold values from 0.25 to 1.75
- layer_norm_bias: float32 [1280], replicated, may hold values from -3 to 3
Outputs:
- grad_patches: bfloat16 [64, 256, 1280], P('dp', None, 'chan')
- grad_w_in: float32 [640, 256], replicated
- grad_w_out: float32 [256, 640], replicated
- grad_b_in: float32 [640], replicated
- grad_gain: float32 [1280], P('chan')
- grad_shift: float32 [1280], P('chan')
All inputs are finite; a program needn't handle non-finite values.
Results may differ from a plain program's by a relative error of at most 0.0065.
Values may be sent and summed in bfloat16 or wider, within the bound.
No kernel may reach another device: no remote copies, remote signals or barrier semaphores. Data moves between devices by JAX's collectives and lax.ppermute only.
A program may use at most 64 MiB of HBM per device.

v0:
```python
import math
import jax
import jax.numpy as jnp
from jax import lax
from jax.sharding import PartitionSpec as P

CHANNEL_COUNT = 1280
eps_norm = 1e-05


def shards(
    patches, cotangent, w_token_in, b_token_in, w_token_out, layer_norm_gain, layer_norm_bias
):
    where = lax.axis_index("chan")
    local_width = patches.shape[2]
    images = float(patches.shape[0] * lax.axis_size("dp"))
    input_float = patches.astype(jnp.float32)
    totals = lax.psum((jnp.sum(input_float, -1), jnp.sum(input_float * input_float, -1)), "chan")
    row_average = totals[0] / CHANNEL_COUNT
    inverse_deviation = lax.rsqrt(totals[1] / CHANNEL_COUNT - row_average * row_average + eps_norm)
    local_gain = lax.dynamic_slice_in_dim(layer_norm_gain, where * local_width, local_width, 0)
    local_bias = lax.dynamic_slice_in_dim(layer_norm_bias, where * local_width, local_width, 0)
    centered_input = (input_float - row_average[..., None]) * inverse_deviation[..., None]
    normalized_output = (centered_input * local_gain + local_bias).astype(jnp.bfloat16)
    pre = (
        jnp.einsum("kp,bpc->bkc", w_token_in, normalized_output, preferred_element_type=jnp.float32)
        + b_token_in[None, :, None]
    )
    cdf = 0.5 * (1.0 + jax.scipy.special.erf(pre / math.sqrt(2.0)))
    act = (pre * cdf).astype(jnp.bfloat16)
    slope = cdf + pre * jnp.exp(-0.5 * pre * pre) / math.sqrt(2.0 * math.pi)
    grad_act = jnp.einsum("pk,bpc->bkc", w_token_out, cotangent, preferred_element_type=jnp.float32)
    grad_pre = (grad_act * slope).astype(jnp.bfloat16)
    gradient_normalized = jnp.einsum(
        "kp,bkc->bpc", w_token_in, grad_pre, preferred_element_type=jnp.float32
    ).astype(jnp.bfloat16)
    dw_out = jnp.einsum("bpc,bkc->pk", cotangent, act, preferred_element_type=jnp.float32)
    dw_in = jnp.einsum(
        "bkc,bpc->kp", grad_pre, normalized_output, preferred_element_type=jnp.float32
    )
    db_in = jnp.sum(grad_pre.astype(jnp.float32), axis=(0, 2))
    summed = lax.psum((dw_in, dw_out, db_in), ("dp", "chan"))
    gradient_block = gradient_normalized.astype(jnp.float32)
    norm_terms = lax.psum(
        (
            jnp.sum(gradient_block * centered_input, axis=(0, 1)),
            jnp.sum(gradient_block, axis=(0, 1)),
        ),
        "dp",
    )
    gradient_centered = gradient_block * local_gain
    sums = lax.psum(
        (jnp.sum(gradient_centered, -1), jnp.sum(gradient_centered * centered_input, -1)), "chan"
    )
    first_term = sums[0] / CHANNEL_COUNT
    second_term = sums[1] / CHANNEL_COUNT
    result = cotangent.astype(jnp.float32) + inverse_deviation[..., None] * (
        gradient_centered - first_term[..., None] - centered_input * second_term[..., None]
    )
    grad_patches = result.astype(jnp.bfloat16)
    return (
        grad_patches,
        summed[0] / images,
        summed[1] / images,
        summed[2] / images,
        norm_terms[0] / images,
        norm_terms[1] / images,
    )


def solution(mesh):
    placed = (P("dp", None, "chan"), P("dp", None, "chan"), P(), P(), P(), P(), P())
    return jax.shard_map(
        shards,
        mesh=mesh,
        in_specs=placed,
        out_specs=(P("dp", None, "chan"), P(), P(), P(), P("chan"), P("chan")),
        check_vma=False,
    )
```

profile of v0, /device:TPU:0, one launch (start us, length us, event | category | flops | bytes accessed | tf_op | source)
XLA Modules:
  0.0 185.8 jit_solution(13512092511223534403)
XLA Ops:
  7.2 0.0 copy-start
  7.2 0.0 all-reduce.6.cloned.1.call-start
  7.2 0.8 dynamic_slice.6
  8.0 0.8 dynamic_slice.7
  8.8 1.7 fusion.24
  10.5 20.5 %all-reduce.3 = (f32[8,256]{1,0:T(8,128)S(1)}, f32[8,256]{1,0:T(8,128)S(1)}) all-reduce(f32[8,256]{1,0:T(8,128)S(1)} %get-tuple-element.16, f32[8,256]{1,0:T(8,128)S(1)} %get-tuple-element.15), channel_id=1, replica_groups=mesh['dp'=8,'chan'=4] {'chan'}, use_global_device_ids=true, to_apply=%region_3.0 | all-reduce | flops 4096 | bytes 32768 | tf_op jit(solution)/shard_map/psum | solution.py:18
  31.1 2.7 %fusion.34 = f32[8,320,640]{2,1,0:T(8,128)S(1)} fusion(bf16[640,256]{1,0:T(8,128)(2,1)S(1)} %copy-done, bf16[8,256,320]{1,2,0:T(8,128)(2,1)} %param.7, f32[320]{0:T(512)S(1)} %dynamic_slice.7, f32[320]{0:T(512)S(1)} %dynamic_slice.6, f32[8,256]{1,0:T(8,128)S(1)} %get-tuple-element.26, f32[8,256]{1,0:T(8,128)S(1)} %get-tuple-element.25), kind=kOutput, calls=%fused_computation.42 | convolution fusion | flops 842792960 | bytes 8210944 | tf_op jit(solution)/shard_map/kp,bpc->bkc/dot_general | solution.py:26
  33.8 2.4 %fusion.30 = f32[256,640]{0,1:T(8,128)} fusion(bf16[8,256,320]{1,2,0:T(8,128)(2,1)S(1)} %copy-done.2, f32[8,320,640]{2,1,0:T(8,128)S(1)} %fusion.34, f32[640]{0:T(1024)S(1)} %copy-done.4), kind=kOutput, calls=%fused_computation.39 | convolution fusion | flops 848691200 | bytes 8522240 | tf_op jit(solution)/shard_map/bpc,bkc->pk/dot_general | solution.py:37
  36.3 3.8 %convert_reduce_fusion = (f32[640]{0:T(1024)S(1)}, bf16[8,640,320]{1,2,0:T(8,128)(2,1)S(1)}) fusion(f32[8,320,640]{2,1,0:T(8,128)S(1)} %fusion.34, f32[640]{0:T(1024)S(1)} %copy-done.4, bf16[8,256,320]{1,2,0:T(8,128)(2,1)S(1)} %copy-done.2, bf16[256,640]{1,0:T(8,128)(2,1)S(1)} %copy-done.3), kind=kOutput, calls=%fused_computation.13 | convolution fusion | flops 860159360 | bytes 11473920 | tf_op jit(solution)/shard_map/pk,bpc->bkc/dot_general | solution.py:32
  40.1 1.7 copy-done.5
  41.8 2.1 %convolution_bitcast_fusion = f32[640,256]{1,0:T(8,128)} fusion(bf16[8,640,320]{1,2,0:T(8,128)(2,1)S(1)} %get-tuple-element.29, bf16[8,256,320]{1,2,0:T(8,128)(2,1)S(1)} %copy-done.1, f32[320]{0:T(512)S(1)} %dynamic_slice.7, f32[320]{0:T(512)S(1)} %dynamic_slice.6, f32[8,256]{1,0:T(8,128)S(1)} %get-tuple-element.26, f32[8,256]{1,0:T(8,128)S(1)} %get-tuple-element.25), kind=kOutput, calls=%fused_computation.40 | convolution fusion | flops 842792960 | bytes 5261824 | tf_op jit(solution)/shard_map/bkc,bpc->kp/dot_general | solution.py:38
  43.9 0.0 all-reduce.6.cloned.1.call-update
  43.9 3.5 %fusion.23 = (f32[320]{0:T(512)S(1)}, f32[8,256]{1,0:T(8,128)S(1)}, f32[8,256]{1,0:T(8,128)S(1)}, bf16[8,320,256]{2,1,0:T(8,128)(2,1)S(1)}) fusion(bf16[8,256,320]{1,2,0:T(8,128)(2,1)S(1)} %copy-done.1, f32[8,256]{1,0:T(8,128)S(1)} %get-tuple-element.26, f32[8,256]{1,0:T(8,128)S(1)} %get-tuple-element.25, f32[320]{0:T(512)S(1)} %dynamic_slice.6, ...), kind=kOutput, calls=%fused_computation.31 | convolution fusion | flops 846065344 | bytes 6261248 | tf_op jit(solution)/shard_map/kp,bkc->bpc/dot_general | solution.py:34
  47.5 38.1 %psum.69 = f32[640]{0:T(1024)S(1)} all-reduce(f32[640]{0:T(1024)S(1)} %get-tuple-element.28), channel_id=1, replica_groups=mesh['dp'=8,'chan'=4] {'dp','chan'}, use_global_device_ids=true, to_apply=%region_11.0 | all-reduce | flops 640 | bytes 5120 | tf_op jit(solution)/shard_map/psum | solution.py:42
  85.5 0.6 broadcast_multiply_fusion.5
  86.1 0.3 convert_reduce_fusion.2
  86.4 12.7 %all-reduce.1 = (f32[320]{0:T(512)S(1)}, f32[320]{0:T(512)S(1)}) all-reduce(f32[320]{0:T(512)S(1)} %get-tuple-element.12, f32[320]{0:T(512)S(1)} %convert_reduce_fusion.2), channel_id=1, replica_groups=mesh['dp'=8,'chan'=4] {'dp'}, use_global_device_ids=true, to_apply=%region_13.0 | all-reduce | flops 640 | bytes 5120 | tf_op jit(solution)/shard_map/psum | solution.py:44
  99.1 0.6 broadcast_multiply_fusion.6
  99.7 18.1 %all-reduce.2 = (f32[8,256]{1,0:T(8,128)S(1)}, f32[8,256]{1,0:T(8,128)S(1)}) all-reduce(f32[8,256]{1,0:T(8,128)S(1)} %get-tuple-element.13, f32[8,256]{1,0:T(8,128)S(1)} %get-tuple-element.14), channel_id=1, replica_groups=mesh['dp'=8,'chan'=4] {'chan'}, use_global_device_ids=true, to_apply=%region_7.0 | all-reduce | flops 4096 | bytes 32768 | tf_op jit(solution)/shard_map/psum | solution.py:52
  117.8 3.4 %fusion.21 = bf16[8,256,320]{1,2,0:T(8,128)(2,1)} fusion(bf16[8,320,256]{2,1,0:T(8,128)(2,1)S(1)} %get-tuple-element.27, bf16[8,256,320]{1,2,0:T(8,128)(2,1)S(1)} %copy-done.1, bf16[8,256,320]{1,2,0:T(8,128)(2,1)} %param.8, f32[8,256]{1,0:T(8,128)S(1)} %get-tuple-element.30, f32[8,256]{1,0:T(8,128)S(1)} %get-tuple-element.31, f32[320]{0:T(512)S(1)} %dynamic_slice.6, ...), kind=kLoop, calls=%fused_computation.29 | loop fusion | flops 7864320 | bytes 5276928 | tf_op jit(solution)/shard_map/convert_element_type | solution.py:60
  121.3 53.5 %all-reduce.6.cloned.1.call-done = (f32[640,256]{1,0:T(8,128)}, f32[256,640]{0,1:T(8,128)}) async-done(((f32[640,256]{1,0:T(8,128)}, f32[256,640]{0,1:T(8,128)}), (f32[640,256]{1,0:T(8,128)}, f32[256,640]{0,1:T(8,128)})) %all-reduce.6.cloned.1.call-update) | async-done | bytes 1310736 | tf_op jit(solution)/shard_map/psum | solution.py:42
  174.8 2.0 %broadcast_multiply_fusion.1 = f32[640,256]{1,0:T(8,128)} fusion(f32[640,256]{1,0:T(8,128)} %get-tuple-element.17), kind=kLoop, calls=%fused_computation.46 | loop fusion | flops 163840 | bytes 1310720 | tf_op jit(solution)/shard_map/div | solution.py:63
  176.8 1.1 broadcast_multiply_fusion
  177.9 1.1 copy.13
  (12 shorter events, 0.0 us)
Async XLA Ops:
  7.2 23.9 %copy-start = (bf16[640,256]{1,0:T(8,128)(2,1)S(1)}, bf16[640,256]{1,0:T(8,128)(2,1)}, u32[]{:S(2)}) copy-start(bf16[640,256]{1,0:T(8,128)(2,1)} %param.9) | copy-start | bytes 983044
  7.2 167.6 %all-reduce.6.cloned.1.call-start = ((), (), s32[]{:S(2)}) async-start(), calls=%async_computation | async-start | bytes 2621440 | tf_op jit(solution)/shard_map/psum | solution.py:42
  31.0 2.8 %copy-start.2 = (bf16[8,256,320]{1,2,0:T(8,128)(2,1)S(1)}, bf16[8,256,320]{1,2,0:T(8,128)(2,1)}, u32[]{:S(2)}) copy-start(bf16[8,256,320]{1,2,0:T(8,128)(2,1)} %param.8) | copy-start | bytes 3932164
  31.1 2.8 %copy-start.4 = (f32[640]{0:T(1024)S(1)}, f32[640]{0:T(1024)}, u32[]{:S(2)}) copy-start(f32[640]{0:T(1024)} %param.10) | copy-start | bytes 7684
  33.8 2.4 %copy-start.3 = (bf16[256,640]{1,0:T(8,128)(2,1)S(1)}, bf16[256,640]{1,0:T(8,128)(2,1)}, u32[]{:S(2)}) copy-start(bf16[256,640]{1,0:T(8,128)(2,1)} %param.11) | copy-start | bytes 983044
  36.3 5.5 %copy-start.1 = (bf16[8,256,320]{1,2,0:T(8,128)(2,1)S(1)}, bf16[8,256,320]{1,2,0:T(8,128)(2,1)}, u32[]{:S(2)}) copy-start(bf16[8,256,320]{1,2,0:T(8,128)(2,1)} %param.7) | copy-start | bytes 3932164
  40.1 1.7 copy-start.5
Sparse Core Ops, SparseCore 0:
  44.1 130.7 all-reduce.5
where the time goes:
time: 186 us
  blocking collectives  89.4 us (48%)
  waiting for transfers between devices  53.5 us (29%)
  matrix products  14.6 us (8%)
  between operations  14.1 us (8%)
  other arithmetic  9.7 us (5%)
  local copies, waits for them, and re-layouts  4.36 us (2%)
    psum x1, waiting for transfers between devices, shards(): summed = lax.psum((dw_in, dw_out, db_in), ('dp', 'chan'))  53.5 us
    psum x1, blocking collectives, shards(): summed = lax.psum((dw_in, dw_out, db_in), ('dp', 'chan'))  38.1 us
    psum x1, blocking collectives, shards(): lax.psum((jnp.sum(input_float, -1), jnp.sum(input_float * input_float, -1...  20.5 us
    psum x1, blocking collectives, shards(): lax.psum((jnp.sum(gradient_centered, -1), jnp.sum(gradient_centered * cen...  18.1 us
    psum x1, blocking collectives, shards(): lax.psum((jnp.sum(gradient_block * centered_input, axis=(0, 1)), jnp.sum(...  12.7 us
    dot_general x1, matrix products, shards(): jnp.einsum('pk,bpc->bkc', w_token_out, cotangent, preferred_element_type=...  3.83 us
  transfers between devices with their start and end apart: 1, of which 1 were waited for; matrix products, arithmetic and copies ran while one was open for 5% of the time, Pallas kernels for 0%

commit v1 on v0

--- a/solution.py
+++ b/solution.py
@@ -39,7 +39,9 @@
         "bkc,bpc->kp", grad_pre, normalized_output, preferred_element_type=jnp.float32
     )
     db_in = jnp.sum(grad_pre.astype(jnp.float32), axis=(0, 2))
-    summed = lax.psum((dw_in, dw_out, db_in), ("dp", "chan"))
+    summed = (dw_in, dw_out, db_in)
+    for axis in ("chan", "dp"):
+        summed = lax.psum(summed, axis)
     gradient_block = gradient_normalized.astype(jnp.float32)
     norm_terms = lax.psum(
         (

time: 186 us -> 175 us (0.941)
  blocking collectives: 89.4 us -> 50.3 us
  waiting for transfers between devices: 53.5 us -> 81.8 us
    psum x2 -> x1, blocking collectives: 50.8 us -> 12.4 us  [shards(): summed = lax.psum(summed, axis)]
    psum x1 -> x2, waiting for transfers between devices: 53.5 us -> 81.8 us  [shards(): summed = lax.psum(summed, axis)]
  transfers between devices with their start and end apart: 1 -> 2, of which waited for: 1 -> 2; matrix products, arithmetic and copies ran while one was open for 5% -> 5% of each run, Pallas kernels for 0% -> 0%
where the time goes in v1:
time: 175 us
  waiting for transfers between devices  81.8 us (47%)
  blocking collectives  50.3 us (29%)
  matrix products  14.6 us (8%)
  between operations  14.1 us (8%)
  other arithmetic  9.69 us (6%)
  local copies, waits for them, and re-layouts  4.36 us (2%)
    psum x2, waiting for transfers between devices, shards(): summed = lax.psum(summed, axis)  81.8 us
    psum x1, blocking collectives, shards(): lax.psum((jnp.sum(input_float, -1), jnp.sum(input_float * input_float, -1...  20.5 us
    psum x1, blocking collectives, shards(): lax.psum((jnp.sum(gradient_centered, -1), jnp.sum(gradient_centered * cen...  17.4 us
    psum x1, blocking collectives, shards(): summed = lax.psum(summed, axis)  12.4 us
    dot_general x1, matrix products, shards(): jnp.einsum('pk,bpc->bkc', w_token_out, cotangent, preferred_element_type=...  3.81 us
    dot_general x1, matrix products, shards(): jnp.einsum('kp,bkc->bpc', w_token_in, grad_pre, preferred_element_type=jn...  3.55 us
  transfers between devices with their start and end apart: 2, of which 2 were waited for; matrix products, arithmetic and copies ran while one was open for 5% of the time, Pallas kernels for 0%

profile of v1, /device:TPU:0, one launch (start us, length us, event | category | flops | bytes accessed | tf_op | source)
XLA Modules:
  0.0 175.0 jit_solution(9042718723528089847)
XLA Ops:
  7.2 0.0 all-reduce.10.cloned.1.call-start
  7.2 0.8 dynamic_slice.6
  8.0 0.8 dynamic_slice.7
  8.8 1.7 fusion.24
  10.5 20.5 %all-reduce.3 = (f32[8,256]{1,0:T(8,128)S(1)}, f32[8,256]{1,0:T(8,128)S(1)}) all-reduce(f32[8,256]{1,0:T(8,128)S(1)} %get-tuple-element.16, f32[8,256]{1,0:T(8,128)S(1)} %get-tuple-element.15), channel_id=1, replica_groups=mesh['dp'=8,'chan'=4] {'chan'}, use_global_device_ids=true, to_apply=%region_3.0 | all-reduce | flops 4096 | bytes 32768 | tf_op jit(solution)/shard_map/psum | solution.py:18
  31.1 2.7 %fusion.34 = f32[8,320,640]{2,1,0:T(8,128)S(1)} fusion(bf16[640,256]{1,0:T(8,128)(2,1)S(1)} %copy-done, bf16[8,256,320]{1,2,0:T(8,128)(2,1)} %param.7, f32[320]{0:T(512)S(1)} %dynamic_slice.7, f32[320]{0:T(512)S(1)} %dynamic_slice.6, f32[8,256]{1,0:T(8,128)S(1)} %get-tuple-element.30, f32[8,256]{1,0:T(8,128)S(1)} %get-tuple-element.29), kind=kOutput, calls=%fused_computation.42 | convolution fusion | flops 842792960 | bytes 8210944 | tf_op jit(solution)/shard_map/kp,bpc->bkc/dot_general | solution.py:26
  33.8 2.4 %fusion.30 = f32[256,640]{0,1:T(8,128)} fusion(bf16[8,256,320]{1,2,0:T(8,128)(2,1)S(1)} %copy-done.2, f32[8,320,640]{2,1,0:T(8,128)S(1)} %fusion.34, f32[640]{0:T(1024)S(1)} %copy-done.4), kind=kOutput, calls=%fused_computation.39 | convolution fusion | flops 848691200 | bytes 8522240 | tf_op jit(solution)/shard_map/bpc,bkc->pk/dot_general | solution.py:37
  36.3 3.8 %convert_reduce_fusion = (f32[640]{0:T(1024)S(1)}, bf16[8,640,320]{1,2,0:T(8,128)(2,1)S(1)}) fusion(f32[8,320,640]{2,1,0:T(8,128)S(1)} %fusion.34, f32[640]{0:T(1024)S(1)} %copy-done.4, bf16[8,256,320]{1,2,0:T(8,128)(2,1)S(1)} %copy-done.2, bf16[256,640]{1,0:T(8,128)(2,1)S(1)} %copy-done.3), kind=kOutput, calls=%fused_computation.13 | convolution fusion | flops 860159360 | bytes 11473920 | tf_op jit(solution)/shard_map/pk,bpc->bkc/dot_general | solution.py:32
  40.1 1.7 copy-done.5
  41.8 2.1 %convolution_bitcast_fusion = f32[640,256]{1,0:T(8,128)} fusion(bf16[8,640,320]{1,2,0:T(8,128)(2,1)S(1)} %get-tuple-element.33, bf16[8,256,320]{1,2,0:T(8,128)(2,1)S(1)} %copy-done.1, f32[320]{0:T(512)S(1)} %dynamic_slice.7, f32[320]{0:T(512)S(1)} %dynamic_slice.6, f32[8,256]{1,0:T(8,128)S(1)} %get-tuple-element.30, f32[8,256]{1,0:T(8,128)S(1)} %get-tuple-element.29), kind=kOutput, calls=%fused_computation.40 | convolution fusion | flops 842792960 | bytes 5261824 | tf_op jit(solution)/shard_map/bkc,bpc->kp/dot_general | solution.py:38
  43.9 0.0 all-reduce.8.cloned.1.call-start
  44.0 3.5 %fusion.23 = (f32[320]{0:T(512)S(1)}, f32[8,256]{1,0:T(8,128)S(1)}, f32[8,256]{1,0:T(8,128)S(1)}, bf16[8,320,256]{2,1,0:T(8,128)(2,1)S(1)}) fusion(bf16[8,256,320]{1,2,0:T(8,128)(2,1)S(1)} %copy-done.1, f32[8,256]{1,0:T(8,128)S(1)} %get-tuple-element.30, f32[8,256]{1,0:T(8,128)S(1)} %get-tuple-element.29, f32[320]{0:T(512)S(1)} %dynamic_slice.6, ...), kind=kOutput, calls=%fused_computation.31 | convolution fusion | flops 846065344 | bytes 6261248 | tf_op jit(solution)/shard_map/kp,bkc->bpc/dot_general | solution.py:34
  47.5 17.4 %all-reduce.2 = (f32[8,256]{1,0:T(8,128)S(1)}, f32[8,256]{1,0:T(8,128)S(1)}, f32[640]{0:T(1024)S(1)}) all-reduce(f32[8,256]{1,0:T(8,128)S(1)} %get-tuple-element.13, f32[8,256]{1,0:T(8,128)S(1)} %get-tuple-element.14, f32[640]{0:T(1024)S(1)} %get-tuple-element.32), channel_id=1, replica_groups=mesh['dp'=8,'chan'=4] {'chan'}, use_global_device_ids=true, to_apply=%region_7.0 | all-reduce | flops 4736 | bytes 37888 | tf_op jit(solution)/shard_map/psum | solution.py:54
  64.9 0.3 convert_reduce_fusion.2
  65.2 12.4 %all-reduce = (f32[640]{0:T(1024)S(1)}, f32[320]{0:T(512)S(1)}, f32[320]{0:T(512)S(1)}) all-reduce(f32[640]{0:T(1024)S(1)} %get-tuple-element.24, f32[320]{0:T(512)S(1)} %get-tuple-element.12, f32[320]{0:T(512)S(1)} %convert_reduce_fusion.2), channel_id=1, replica_groups=mesh['dp'=8,'chan'=4] {'dp'}, use_global_device_ids=true, to_apply=%region_14.0 | all-reduce | flops 1280 | bytes 10240 | tf_op jit(solution)/shard_map/psum | solution.py:44
  77.6 0.6 broadcast_multiply_fusion.5
  78.2 25.1 %all-reduce.10.cloned.1.call-done = (f32[640,256]{1,0:T(8,128)}, f32[256,640]{0,1:T(8,128)}) async-done(((f32[640,256]{1,0:T(8,128)}, f32[256,640]{0,1:T(8,128)}), (f32[640,256]{1,0:T(8,128)}, f32[256,640]{0,1:T(8,128)})) %all-reduce.10.cloned.1.call-update) | async-done | bytes 1310736 | tf_op jit(solution)/shard_map/psum | solution.py:44
  103.2 0.0 all-reduce.8.cloned.1.call-update
  103.3 0.6 broadcast_multiply_fusion.6
  103.9 3.4 %fusion.21 = bf16[8,256,320]{1,2,0:T(8,128)(2,1)} fusion(bf16[8,320,256]{2,1,0:T(8,128)(2,1)S(1)} %get-tuple-element.31, bf16[8,256,320]{1,2,0:T(8,128)(2,1)S(1)} %copy-done.1, bf16[8,256,320]{1,2,0:T(8,128)(2,1)} %param.8, f32[8,256]{1,0:T(8,128)S(1)} %get-tuple-element.34, f32[8,256]{1,0:T(8,128)S(1)} %get-tuple-element.35, f32[320]{0:T(512)S(1)} %dynamic_slice.6, ...), kind=kLoop, calls=%fused_computation.29 | loop fusion | flops 7864320 | bytes 5276928 | tf_op jit(solution)/shard_map/convert_element_type | solution.py:62
  107.3 56.7 %all-reduce.8.cloned.1.call-done = (f32[640,256]{1,0:T(8,128)}, f32[256,640]{0,1:T(8,128)}) async-done(((f32[640,256]{1,0:T(8,128)}, f32[256,640]{0,1:T(8,128)}), (f32[640,256]{1,0:T(8,128)}, f32[256,640]{0,1:T(8,128)})) %all-reduce.8.cloned.1.call-update) | async-done | bytes 1310736 | tf_op jit(solution)/shard_map/psum | solution.py:44
  164.0 2.0 %broadcast_multiply_fusion.1 = f32[640,256]{1,0:T(8,128)} fusion(f32[640,256]{1,0:T(8,128)} %get-tuple-element.20), kind=kLoop, calls=%fused_computation.46 | loop fusion | flops 163840 | bytes 1310720 | tf_op jit(solution)/shard_map/div | solution.py:65
  166.0 1.1 broadcast_multiply_fusion
  167.1 1.1 copy.13
  (14 shorter events, 0.1 us)
Async XLA Ops:
  7.2 23.9 %copy-start = (bf16[640,256]{1,0:T(8,128)(2,1)S(1)}, bf16[640,256]{1,0:T(8,128)(2,1)}, u32[]{:S(2)}) copy-start(bf16[640,256]{1,0:T(8,128)(2,1)} %param.9) | copy-start | bytes 983044
  7.2 96.1 %all-reduce.10.cloned.1.call-start = ((), (), s32[]{:S(2)}) async-start(), calls=%async_computation.1 | async-start | bytes 2621440 | tf_op jit(solution)/shard_map/psum | solution.py:44
  31.0 2.8 %copy-start.2 = (bf16[8,256,320]{1,2,0:T(8,128)(2,1)S(1)}, bf16[8,256,320]{1,2,0:T(8,128)(2,1)}, u32[]{:S(2)}) copy-start(bf16[8,256,320]{1,2,0:T(8,128)(2,1)} %param.8) | copy-start | bytes 3932164
  31.1 2.8 %copy-start.4 = (f32[640]{0:T(1024)S(1)}, f32[640]{0:T(1024)}, u32[]{:S(2)}) copy-start(f32[640]{0:T(1024)} %param.10) | copy-start | bytes 7684
  33.8 2.4 %copy-start.3 = (bf16[256,640]{1,0:T(8,128)(2,1)S(1)}, bf16[256,640]{1,0:T(8,128)(2,1)}, u32[]{:S(2)}) copy-start(bf16[256,640]{1,0:T(8,128)(2,1)} %param.11) | copy-start | bytes 983044
  36.3 5.5 %copy-start.1 = (bf16[8,256,320]{1,2,0:T(8,128)(2,1)S(1)}, bf16[8,256,320]{1,2,0:T(8,128)(2,1)}, u32[]{:S(2)}) copy-start(bf16[8,256,320]{1,2,0:T(8,128)(2,1)} %param.7) | copy-start | bytes 3932164
  40.1 1.7 copy-start.5
  43.9 120.1 %all-reduce.8.cloned.1.call-start = ((), (), s32[]{:S(2)}) async-start(), calls=%async_computation | async-start | bytes 2621440 | tf_op jit(solution)/shard_map/psum | solution.py:44
Sparse Core Ops, SparseCore 0:
  44.0 59.1 all-reduce.9
  106.5 57.4 all-reduce.7
